TPU v7x, 32 devices: a whole 2x2x4 slice. The times are simulated.
32 devices in a mesh: row: 16 (over z, y, x), col: 2 (over core).
Axes of the slice: x: 2, y: 2, z: 4, core: 2. Of those that a mesh axis runs over, the one named last changes fastest.
Arguments:
- matrix: float32 [2, 16, 4, 2, 256, 256], P(None, 'row', None, 'col'), as said below
- keep_mask: int32 [2, 16, 4, 2], P(None, 'row', None, 'col'), may hold values 0 or 1
Outputs:
- factored: float32 [2, 16, 4, 2, 256, 256], P(None, 'row', None, 'col')
Inputs may be any that keep to these rules, and one draw needn't show every extreme that they name: `matrix`: tiles whose row and column index are equal are symmetric, and the symmetric completion of the kept tiles in the window's leading two tile rows and columns is positive definite, so that both panel steps meet positive definite diagonal tiles.
All inputs are finite; a program needn't handle non-finite values. No bound on the sum of `keep_mask` on one device may be relied on, other than what follows from the above.
Results may differ from a plain program's by a relative error of at most 0.0001.
Values sent between devices are 32-bit elements; how exact they have to be, the bound alone decides.
No kernel may reach another device: no remote copies, remote signals or barrier semaphores. Data moves between devices by JAX's collectives and lax.ppermute only.
A program may use at most 64 MiB of HBM per device.

v0:
```python
import jax
import jax.numpy as jnp
from jax import lax
from jax.sharding import PartitionSpec as P

HALF_BAND = 256


def broadcast(shard, axis, root):
    mine = lax.axis_index(axis) == root
    return lax.psum(jnp.where(mine, shard, jnp.zeros_like(shard)), axis)


def right_solve(factor_diag, blocks):
    block_count, tile_edge = (blocks.shape[0], blocks.shape[1])
    stacked = jnp.transpose(blocks, (2, 0, 1)).reshape(tile_edge, block_count * tile_edge)
    solved = lax.linalg.triangular_solve(factor_diag, stacked, left_side=True, lower=True)
    return jnp.transpose(solved.reshape(tile_edge, block_count, tile_edge), (1, 2, 0))


def local(matrix, keep_mask):
    blocks = matrix[:, 0, :, 0]
    kept_marks = keep_mask[:, 0, :, 0]
    row_count, pair_count, tile_edge = (blocks.shape[0], blocks.shape[1], blocks.shape[-1])
    row_devices = lax.axis_size("row")
    row_place = lax.axis_index("row")
    col_place = lax.axis_index("col")
    tile_row = jnp.arange(row_count, dtype=jnp.int32)[:, None] * row_devices + row_place
    tile_col = 2 * jnp.arange(pair_count, dtype=jnp.int32)[None, :] + col_place
    kept_tile = (
        ((kept_marks == 1) | (tile_row == tile_col))
        & (tile_row >= tile_col)
        & (tile_row - tile_col <= HALF_BAND)
    )
    blocks = jnp.where(kept_tile[:, :, None, None], blocks, 0.0)
    lower_part = tile_row >= tile_col
    identity = jnp.eye(tile_edge, dtype=jnp.float32)
    row_index = tile_row[:, 0][:, None, None]
    for panel_step in range(2):
        diag_block = broadcast(blocks[0, 0], "row", panel_step)
        factor_diag = jnp.linalg.cholesky(jnp.where(col_place == panel_step, diag_block, identity))
        solved = right_solve(factor_diag, blocks[:, 0])
        factor_panel_col = jnp.where(
            row_index > panel_step,
            solved,
            jnp.where(row_index == panel_step, factor_diag[None], 0.0),
        )
        factor_panel_col = broadcast(factor_panel_col, "col", panel_step)
        unused = jnp.zeros((tile_edge, tile_edge), jnp.float32)
        leading = [unused for source in range(panel_step + 1)]
        trailing = [
            broadcast(factor_panel_col[0], "row", source)
            for source in range(panel_step + 1, 2 * pair_count)
        ]
        factor_column_set = jnp.stack(leading + trailing)
        column = jnp.where(col_place == panel_step, factor_panel_col, blocks[:, 0])
        blocks = blocks.at[:, 0].set(column)
        paired = factor_column_set.reshape(pair_count, 2, tile_edge, tile_edge)
        my_columns = jnp.where(col_place == 0, paired[:, 0], paired[:, 1])
        product = jnp.einsum(
            "tab,scb->tsac",
            factor_panel_col,
            my_columns,
            precision=lax.Precision.HIGHEST,
            preferred_element_type=jnp.float32,
        )
        selected = (lower_part & (tile_col > panel_step))[:, 0:pair_count, None, None]
        updated = blocks - jnp.where(selected, product, 0.0)
        blocks = jnp.concatenate([blocks[:, :0], updated, blocks[:, pair_count:]], axis=1)
    return blocks[:, None, :, None]


def solution(mesh):
    return jax.shard_map(
        local,
        mesh=mesh,
        in_specs=(P(None, "row", None, "col", None, None), P(None, "row", None, "col")),
        out_specs=P(None, "row", None, "col", None, None),
        check_vma=False,
    )
```

profile of v0, /device:TPU:0, one launch (start us, length us, event | category | flops | bytes accessed | tf_op | source)
XLA Modules:
  0.0 718.5 jit_solution(1143109675651483619)
XLA Ops:
  6.6 2.9 copy.20
  13.8 108.2 %all-reduce.10.cloned.1.call-done = f32[256,256]{0,1:T(8,128)} async-done(((f32[256,256]{0,1:T(8,128)}), f32[256,256]{0,1:T(8,128)}) %all-reduce.10.cloned.1.call-update) | async-done | bytes 262160 | tf_op jit(solution)/shard_map/psum | solution.py:11
  125.6 11.7 %cholesky.130 = f32[128,128]{1,0:T(8,128)S(1)} custom-call(f32[128,128]{1,0:T(8,128)S(1)} %cholesky.194), custom_call_target="Cholesky" | custom-call | tf_op jit(solution)/shard_map/jit(cholesky)/cholesky | solution.py:41
  137.9 9.8 %custom-call.13 = f32[1,128,128]{1,2,0:T(8,128)S(1)} custom-call(f32[1,128,128]{2,1,0:T(8,128)S(1)} %get-tuple-element.112), custom_call_target="InvertDiagBlocksLowerTriangular" | custom-call | tf_op jit(solution)/shard_map/jit(cholesky)/cholesky | solution.py:41
  149.9 11.7 %cholesky.147 = f32[128,128]{1,0:T(8,128)S(1)} custom-call(f32[128,128]{1,0:T(8,128)S(1)} %convolution_subtract_fusion.3), custom_call_target="Cholesky" | custom-call | tf_op jit(solution)/shard_map/jit(cholesky)/cholesky | solution.py:41
  168.1 5.5 while.6
  174.2 20.5 %custom-call.14 = f32[2,128,128]{1,2,0:T(8,128)S(1)} custom-call(f32[2,128,128]{2,1,0:T(8,128)} %copy-done.13), custom_call_target="InvertDiagBlocksLowerTriangular" | custom-call | tf_op jit(solution)/shard_map/triangular_solve/custom-call.0 | solution.py:17
  201.3 17.8 %all-reduce.12.cloned.1.call-done = f32[2,256,256]{1,2,0:T(8,128)} async-done(((f32[2,256,256]{1,2,0:T(8,128)}), f32[2,256,256]{1,2,0:T(8,128)}) %all-reduce.12.cloned.1.call-update) | async-done | bytes 524304 | tf_op jit(solution)/shard_map/psum | solution.py:11
  222.3 129.0 %all-reduce.20.cloned.1.call-done = (f32[1,256,256]{1,2,0:T(8,128)}, f32[1,256,256]{1,2,0:T(8,128)}, f32[1,256,256]{1,2,0:T(8,128)}, f32[1,256,256]{1,2,0:T(8,12...) async-done(((f32[1,256,256]{1,2,0:T(8,128)}, f32[1,256,256]{1,2,0:T(8,128)}, f32[1,256,256]{1,2,0:T(8,128)}, f32[1,256,256]{1,2,0:T(8,128)}, ...) | async-done | bytes 1835024 | tf_op jit(solution)/shard_map/psum | solution.py:11
  360.2 3.0 fusion.44
  364.8 2.5 copy.54
  367.3 3.0 fusion.2
  374.0 104.6 %all-reduce.14.cloned.1.call-done = f32[256,256]{0,1:T(8,128)} async-done(((f32[256,256]{0,1:T(8,128)}), f32[256,256]{0,1:T(8,128)}) %all-reduce.14.cloned.1.call-update) | async-done | bytes 262160 | tf_op jit(solution)/shard_map/psum | solution.py:11
  478.8 11.7 %cholesky.164 = f32[128,128]{1,0:T(8,128)S(1)} custom-call(f32[128,128]{1,0:T(8,128)S(1)} %cholesky.197), custom_call_target="Cholesky" | custom-call | tf_op jit(solution)/shard_map/jit(cholesky)/cholesky | solution.py:41
  490.5 9.8 %custom-call.15 = f32[1,128,128]{1,2,0:T(8,128)S(1)} custom-call(f32[1,128,128]{2,1,0:T(8,128)S(1)} %get-tuple-element.108), custom_call_target="InvertDiagBlocksLowerTriangular" | custom-call | tf_op jit(solution)/shard_map/jit(cholesky)/cholesky | solution.py:41
  500.8 11.7 %cholesky.181 = f32[128,128]{1,0:T(8,128)S(1)} custom-call(f32[128,128]{1,0:T(8,128)S(1)} %convolution_subtract_fusion.2), custom_call_target="Cholesky" | custom-call | tf_op jit(solution)/shard_map/jit(cholesky)/cholesky | solution.py:41
  515.5 4.5 while.7
  520.0 19.7 %custom-call.16 = f32[2,128,128]{1,2,0:T(8,128)S(1)} custom-call(f32[2,128,128]{2,1,0:T(8,128)S(1)} %get-tuple-element.46), custom_call_target="InvertDiagBlocksLowerTriangular" | custom-call | tf_op jit(solution)/shard_map/triangular_solve/custom-call.0 | solution.py:17
  542.8 17.8 %all-reduce.16.cloned.1.call-done = f32[2,256,256]{1,2,0:T(8,128)} async-done(((f32[2,256,256]{1,2,0:T(8,128)}), f32[2,256,256]{1,2,0:T(8,128)}) %all-reduce.16.cloned.1.call-update) | async-done | bytes 524304 | tf_op jit(solution)/shard_map/psum | solution.py:11
  563.8 125.2 %all-reduce.18.cloned.1.call-done = (f32[1,256,256]{1,2,0:T(8,128)}, f32[1,256,256]{1,2,0:T(8,128)}, f32[1,256,256]{1,2,0:T(8,128)}, f32[1,256,256]{1,2,0:T(8,12...) async-done(((f32[1,256,256]{1,2,0:T(8,128)}, f32[1,256,256]{1,2,0:T(8,128)}, f32[1,256,256]{1,2,0:T(8,128)}, f32[1,256,256]{1,2,0:T(8,128)}, f32[1,256,256]{1,2,0:T(8,128)}, ...) | async-done | bytes 1572880 | tf_op jit(solution)/shard_map/psum | solution.py:11
  697.2 3.0 fusion.42
  701.7 2.5 copy.57
  704.3 4.3 fusion.1
  708.5 2.9 copy.42
  (135 shorter events, 67.5 us)
Async XLA Ops:
  6.5 115.5 %all-reduce.10.cloned.1.call-start = ((), (), s32[]{:S(2)}) async-start(), calls=%async_computation | async-start | bytes 524288 | tf_op jit(solution)/shard_map/psum | solution.py:11
  6.5 2.9 copy-start.14
  12.2 207.0 %all-reduce.12.cloned.1.call-start = ((), (), s32[]{:S(2)}) async-start(), calls=%async_computation.1 | async-start | bytes 1048576 | tf_op jit(solution)/shard_map/psum | solution.py:11
  123.0 71.7 %copy-start.4 = (f32[256,2,256]{0,2,1:T(8,128)S(1)}, f32[256,2,256]{0,2,1:T(8,128)}, u32[]{:S(2)}) copy-start(f32[256,2,256]{0,2,1:T(8,128)} %copy.23) | copy-start | bytes 1572868
  124.9 0.7 copy-start.7
  163.0 2.1 copy-start.5
  173.6 0.6 copy-start.13
  195.8 2.7 copy-start.6
  201.2 150.1 %all-reduce.20.cloned.1.call-start = ((), (), s32[]{:S(2)}) async-start(), calls=%async_computation.5 | async-start | bytes 3670016 | tf_op jit(solution)/shard_map/psum | solution.py:11
  219.1 3.1 copy-start.2
  221.4 257.1 %all-reduce.14.cloned.1.call-start = ((), (), s32[]{:S(2)}) async-start(), calls=%async_computation.2 | async-start | bytes 524288 | tf_op jit(solution)/shard_map/psum | solution.py:11
  351.3 6.8 copy-start.10
  351.3 7.5 %copy-start.9 = (f32[1,256,256]{1,2,0:T(8,128)S(1)}, f32[1,256,256]{1,2,0:T(8,128)}, u32[]{:S(2)}) copy-start(f32[1,256,256]{1,2,0:T(8,128)} %get-tuple-element.74) | copy-start | bytes 786436
  351.3 8.2 %copy-start.8 = (f32[1,256,256]{1,2,0:T(8,128)S(1)}, f32[1,256,256]{1,2,0:T(8,128)}, u32[]{:S(2)}) copy-start(f32[1,256,256]{1,2,0:T(8,128)} %get-tuple-element.75) | copy-start | bytes 786436
  370.3 1.3 copy-start
  372.4 188.2 %all-reduce.16.cloned.1.call-start = ((), (), s32[]{:S(2)}) async-start(), calls=%async_computation.3 | async-start | bytes 1048576 | tf_op jit(solution)/shard_map/psum | solution.py:11
  373.9 141.5 %copy-start.15 = (s32[2,2]{1,0:T(2,128)S(1)}, s32[2,2]{1,0:T(2,128)}, u32[]{:S(2)}) copy-start(s32[2,2]{1,0:T(2,128)} %get-tuple-element.288) | copy-start | bytes 52
  542.7 21.0 %copy-start.1 = (f32[2,4,256,256]{2,3,1,0:T(8,128)S(1)}, f32[2,4,256,256]{2,3,1,0:T(8,128)}, u32[]{:S(2)}) copy-start(f32[2,4,256,256]{2,3,1,0:T(8,128)} %copy-done) | copy-start | bytes 6291460
  542.7 146.3 %all-reduce.18.cloned.1.call-start = ((), (), s32[]{:S(2)}) async-start(), calls=%async_computation.4 | async-start | bytes 3145728 | tf_op jit(solution)/shard_map/psum | solution.py:11
  560.6 3.1 copy-start.3
  689.0 6.7 copy-start.12
  689.0 7.5 %copy-start.11 = (f32[1,256,256]{1,2,0:T(8,128)S(1)}, f32[1,256,256]{1,2,0:T(8,128)}, u32[]{:S(2)}) copy-start(f32[1,256,256]{1,2,0:T(8,128)} %get-tuple-element.68) | copy-start | bytes 786436
Sparse Core Ops, SparseCore 0:
  12.6 109.3 all-reduce.9
  201.4 17.7 all-reduce.11
  225.6 125.6 all-reduce.19
  372.5 105.9 all-reduce.13
  542.8 17.7 all-reduce.15
  567.9 121.0 all-reduce.17
where the time goes:
time: 728 us; the launch traced here: 718 us
  waiting for transfers between devices  503 us (69%)
  other arithmetic  126 us (17%)
  local copies, waits for them, and re-layouts  58.8 us (8%)
  between operations  16.9 us (2%)
  matrix products  12.7 us (2%)
    psum x6, waiting for transfers between devices, broadcast(): return lax.psum(jnp.where(mine, shard, jnp.zeros_like(shard)), axis)  503 us
    another operation x14, other arithmetic, local(): jnp.linalg.cholesky(jnp.where(col_place == panel_step, diag_block, identi...  70.6 us
    another operation x7, other arithmetic, right_solve(): lax.linalg.triangular_solve(factor_diag, stacked, left_side=True, lower=T...  42.5 us
    unnamed x50, local copies, waits for them, and re-layouts  31 us
  transfers between devices with their start and end apart: 6, of which 6 were waited for; matrix products, arithmetic and copies ran while one was open for 1% of the time, Pallas kernels for 0%

commit v1 on v0

--- a/solution.py
+++ b/solution.py
@@ -8,7 +8,7 @@
 
 def broadcast(shard, axis, root):
     mine = lax.axis_index(axis) == root
-    return lax.psum(jnp.where(mine, shard, jnp.zeros_like(shard)), axis)
+    return jnp.sum(lax.all_gather(jnp.where(mine, shard, jnp.zeros_like(shard)), axis), axis=0)
 
 
 def right_solve(factor_diag, blocks):

time: 728 us -> 1370 us (1.88)
  waiting for transfers between devices: 503 us -> 1130 us
  other arithmetic: 126 us -> 164 us
  local copies, waits for them, and re-layouts: 58.8 us -> 24.4 us
    all_gather x0 -> x17, waiting for transfers between devices: none -> 1130 us  [broadcast(): lax.all_gather(jnp.where(mine, shard, jnp.zeros_like(shard)), axis)]
    psum x6 -> x0, waiting for transfers between devices: 503 us -> none  [broadcast(): return lax.psum(jnp.where(mine, shard, jnp.zeros_like(shard)), axis)]
    reduce_sum x0 -> x17, other arithmetic: none -> 41.2 us  [broadcast(): jnp.sum(lax.all_gather(jnp.where(mine, shard, jnp.zeros_like(shard)), axi...]
    unnamed x50 -> x23, local copies, waits for them, and re-layouts: 31 us -> 10.7 us
  transfers between devices with their start and end apart: 6 -> 17, of which waited for: 6 -> 17; matrix products, arithmetic and copies ran while one was open for 1% -> 3% of each run, Pallas kernels for 0% -> 0%
where the time goes in v1:
time: 1370 us; the launch traced here: 1360 us
  waiting for transfers between devices  1130 us (82%)
  other arithmetic  164 us (12%)
  local copies, waits for them, and re-layouts  24.4 us (2%)
  between operations  16.7 us (1%)
  matrix products  14.4 us (1%)
    all_gather x17, waiting for transfers between devices, broadcast(): lax.all_gather(jnp.where(mine, shard, jnp.zeros_like(shard)), axis)  1130 us
    another operation x14, other arithmetic, local(): jnp.linalg.cholesky(jnp.where(col_place == panel_step, diag_block, identi...  69.3 us
    reduce_sum x17, other arithmetic, broadcast(): jnp.sum(lax.all_gather(jnp.where(mine, shard, jnp.zeros_like(shard)), axi...  41.2 us
    another operation x7, other arithmetic, right_solve(): lax.linalg.triangular_solve(factor_diag, stacked, left_side=True, lower=T...  40.9 us
  transfers between devices with their start and end apart: 17, of which 17 were waited for; matrix products, arithmetic and copies ran while one was open for 3% of the time, Pallas kernels for 0%

profile of v1, /device:TPU:0, one launch (start us, length us, event | category | flops | bytes accessed | tf_op | source)
XLA Modules:
  0.0 1355.7 jit_solution(3204495361882074598)
XLA Ops:
  10.4 78.6 %all-gather.48.cloned.1.call-done = f32[16,1,256,256]{3,2,1,0:T(8,128)} async-done(((f32[1,1,256,256]{3,2,1,0:T(8,128)}), f32[16,1,256,256]{3,2,1,0:T(8,128)}) %all-gather.48.cloned.1.call-update) | async-done | bytes 4194320 | tf_op jit(solution)/shard_map/all_gather | solution.py:11
  93.5 11.7 cholesky.130
  106.0 9.8 custom-call.13
  118.0 11.7 cholesky.147
  137.0 19.7 %custom-call.14 = f32[2,128,128]{1,2,0:T(8,128)S(1)} custom-call(f32[2,128,128]{2,1,0:T(8,128)S(1)} %get-tuple-element.45), custom_call_target="InvertDiagBlocksLowerTriangular" | custom-call | tf_op jit(solution)/shard_map/triangular_solve/custom-call.0 | solution.py:17
  175.4 72.4 %all-gather.24.cloned.1.call-done = f32[16,256,256]{2,1,0:T(8,128)} async-done(((f32[1,256,256]{2,1,0:T(8,128)}), f32[16,256,256]{2,1,0:T(8,128)}) %all-gather.24.cloned.1.call-update) | async-done | bytes 4194320 | tf_op jit(solution)/shard_map/all_gather | solution.py:11
  250.4 74.9 %all-gather.26.cloned.1.call-done = f32[16,256,256]{2,1,0:T(8,128)} async-done(((f32[1,256,256]{2,1,0:T(8,128)}), f32[16,256,256]{2,1,0:T(8,128)}) %all-gather.26.cloned.1.call-update) | async-done | bytes 4194320 | tf_op jit(solution)/shard_map/all_gather | solution.py:11
  327.7 74.9 %all-gather.28.cloned.1.call-done = f32[16,256,256]{2,1,0:T(8,128)} async-done(((f32[1,256,256]{2,1,0:T(8,128)}), f32[16,256,256]{2,1,0:T(8,128)}) %all-gather.28.cloned.1.call-update) | async-done | bytes 4194320 | tf_op jit(solution)/shard_map/all_gather | solution.py:11
  405.0 74.9 %all-gather.30.cloned.1.call-done = f32[16,256,256]{2,1,0:T(8,128)} async-done(((f32[1,256,256]{2,1,0:T(8,128)}), f32[16,256,256]{2,1,0:T(8,128)}) %all-gather.30.cloned.1.call-update) | async-done | bytes 4194320 | tf_op jit(solution)/shard_map/all_gather | solution.py:11
  482.4 75.0 %all-gather.32.cloned.1.call-done = f32[16,256,256]{2,1,0:T(8,128)} async-done(((f32[1,256,256]{2,1,0:T(8,128)}), f32[16,256,256]{2,1,0:T(8,128)}) %all-gather.32.cloned.1.call-update) | async-done | bytes 4194320 | tf_op jit(solution)/shard_map/all_gather | solution.py:11
  559.8 75.0 %all-gather.22.cloned.1.call-done = f32[16,256,256]{2,1,0:T(8,128)} async-done(((f32[1,256,256]{2,1,0:T(8,128)}), f32[16,256,256]{2,1,0:T(8,128)}) %all-gather.22.cloned.1.call-update) | async-done | bytes 4194320 | tf_op jit(solution)/shard_map/all_gather | solution.py:11
  641.6 70.7 %all-gather.34.cloned.1.call-done = f32[16,256,256]{2,1,0:T(8,128)} async-done(((f32[1,256,256]{2,1,0:T(8,128)}), f32[16,256,256]{2,1,0:T(8,128)}) %all-gather.34.cloned.1.call-update) | async-done | bytes 4194320 | tf_op jit(solution)/shard_map/all_gather | solution.py:11
  720.9 74.4 %all-gather.52.cloned.1.call-done = f32[16,1,256,256]{3,2,1,0:T(8,128)} async-done(((f32[1,1,256,256]{3,2,1,0:T(8,128)}), f32[16,1,256,256]{3,2,1,0:T(8,128)}) %all-gather.52.cloned.1.call-update) | async-done | bytes 4194320 | tf_op jit(solution)/shard_map/all_gather | solution.py:11
  799.8 11.7 cholesky.164
  812.3 9.8 custom-call.15
  824.3 11.7 cholesky.181
  843.0 19.7 %custom-call.16 = f32[2,128,128]{1,2,0:T(8,128)S(1)} custom-call(f32[2,128,128]{2,1,0:T(8,128)S(1)} %get-tuple-element.46), custom_call_target="InvertDiagBlocksLowerTriangular" | custom-call | tf_op jit(solution)/shard_map/triangular_solve/custom-call.0 | solution.py:17
  866.1 7.7 all-gather.54.cloned.1.call-done
  880.6 73.3 %all-gather.38.cloned.1.call-done = f32[16,256,256]{2,1,0:T(8,128)} async-done(((f32[1,256,256]{2,1,0:T(8,128)}), f32[16,256,256]{2,1,0:T(8,128)}) %all-gather.38.cloned.1.call-update) | async-done | bytes 4194320 | tf_op jit(solution)/shard_map/all_gather | solution.py:11
  956.3 75.0 %all-gather.40.cloned.1.call-done = f32[16,256,256]{2,1,0:T(8,128)} async-done(((f32[1,256,256]{2,1,0:T(8,128)}), f32[16,256,256]{2,1,0:T(8,128)}) %all-gather.40.cloned.1.call-update) | async-done | bytes 4194320 | tf_op jit(solution)/shard_map/all_gather | solution.py:11
  1033.8 74.9 %all-gather.42.cloned.1.call-done = f32[16,256,256]{2,1,0:T(8,128)} async-done(((f32[1,256,256]{2,1,0:T(8,128)}), f32[16,256,256]{2,1,0:T(8,128)}) %all-gather.42.cloned.1.call-update) | async-done | bytes 4194320 | tf_op jit(solution)/shard_map/all_gather | solution.py:11
  1111.2 74.9 %all-gather.44.cloned.1.call-done = f32[16,256,256]{2,1,0:T(8,128)} async-done(((f32[1,256,256]{2,1,0:T(8,128)}), f32[16,256,256]{2,1,0:T(8,128)}) %all-gather.44.cloned.1.call-update) | async-done | bytes 4194320 | tf_op jit(solution)/shard_map/all_gather | solution.py:11
  1189.2 74.2 %all-gather.36.cloned.1.call-done = f32[16,256,256]{2,1,0:T(8,128)} async-done(((f32[1,256,256]{2,1,0:T(8,128)}), f32[16,256,256]{2,1,0:T(8,128)}) %all-gather.36.cloned.1.call-update) | async-done | bytes 4194320 | tf_op jit(solution)/shard_map/all_gather | solution.py:11
  1271.2 69.6 %all-gather.46.cloned.1.call-done = f32[16,256,256]{2,1,0:T(8,128)} async-done(((f32[1,256,256]{2,1,0:T(8,128)}), f32[16,256,256]{2,1,0:T(8,128)}) %all-gather.46.cloned.1.call-update) | async-done | bytes 4194320 | tf_op jit(solution)/shard_map/all_gather | solution.py:11
  (157 shorter events, 120.8 us)
Async XLA Ops:
  6.5 82.5 %all-gather.48.cloned.1.call-start = ((), (), s32[]{:S(2)}) async-start(), calls=%async_computation.13 | async-start | bytes 4456448 | tf_op jit(solution)/shard_map/all_gather | solution.py:11
  10.1 157.7 %all-gather.50.cloned.1.call-start = ((), (), s32[]{:S(2)}) async-start(), calls=%async_computation.14 | async-start | bytes 1572864 | tf_op jit(solution)/shard_map/all_gather | solution.py:11
  93.5 12.5 copy-start.2
  160.0 87.9 %all-gather.24.cloned.1.call-start = ((), (), s32[]{:S(2)}) async-start(), calls=%async_computation.1 | async-start | bytes 4456448 | tf_op jit(solution)/shard_map/all_gather | solution.py:11
  170.5 154.7 %all-gather.26.cloned.1.call-start = ((), (), s32[]{:S(2)}) async-start(), calls=%async_computation.2 | async-start | bytes 4456448 | tf_op jit(solution)/shard_map/all_gather | solution.py:11
  171.0 231.5 %all-gather.28.cloned.1.call-start = ((), (), s32[]{:S(2)}) async-start(), calls=%async_computation.3 | async-start | bytes 4456448 | tf_op jit(solution)/shard_map/all_gather | solution.py:11
  171.6 308.3 %all-gather.30.cloned.1.call-start = ((), (), s32[]{:S(2)}) async-start(), calls=%async_computation.4 | async-start | bytes 4456448 | tf_op jit(solution)/shard_map/all_gather | solution.py:11
  172.2 385.2 %all-gather.32.cloned.1.call-start = ((), (), s32[]{:S(2)}) async-start(), calls=%async_computation.5 | async-start | bytes 4456448 | tf_op jit(solution)/shard_map/all_gather | solution.py:11
  173.0 461.9 %all-gather.22.cloned.1.call-start = ((), (), s32[]{:S(2)}) async-start(), calls=%async_computation | async-start | bytes 4456448 | tf_op jit(solution)/shard_map/all_gather | solution.py:11
  173.7 538.6 %all-gather.34.cloned.1.call-start = ((), (), s32[]{:S(2)}) async-start(), calls=%async_computation.6 | async-start | bytes 4456448 | tf_op jit(solution)/shard_map/all_gather | solution.py:11
  174.4 620.9 %all-gather.52.cloned.1.call-start = ((), (), s32[]{:S(2)}) async-start(), calls=%async_computation.15 | async-start | bytes 4456448 | tf_op jit(solution)/shard_map/all_gather | solution.py:11
  175.4 74.9 %copy-start = (f32[2,4,256,256]{3,2,0,1:T(8,128)}, f32[2,4,256,256]{3,2,0,1:T(8,128)S(1)}, u32[]{:S(2)}) copy-start(f32[2,4,256,256]{3,2,0,1:T(8,128)S(1)} %fusion.12) | copy-start | bytes 6291460
  720.5 153.3 %all-gather.54.cloned.1.call-start = ((), (), s32[]{:S(2)}) async-start(), calls=%async_computation.16 | async-start | bytes 1572864 | tf_op jit(solution)/shard_map/all_gather | solution.py:11
  799.8 12.5 copy-start.3
  866.0 87.9 %all-gather.38.cloned.1.call-start = ((), (), s32[]{:S(2)}) async-start(), calls=%async_computation.8 | async-start | bytes 4456448 | tf_op jit(solution)/shard_map/all_gather | solution.py:11
  876.5 154.9 %all-gather.40.cloned.1.call-start = ((), (), s32[]{:S(2)}) async-start(), calls=%async_computation.9 | async-start | bytes 4456448 | tf_op jit(solution)/shard_map/all_gather | solution.py:11
  877.2 231.5 %all-gather.42.cloned.1.call-start = ((), (), s32[]{:S(2)}) async-start(), calls=%async_computation.10 | async-start | bytes 4456448 | tf_op jit(solution)/shard_map/all_gather | solution.py:11
  877.8 308.2 %all-gather.44.cloned.1.call-start = ((), (), s32[]{:S(2)}) async-start(), calls=%async_computation.11 | async-start | bytes 4456448 | tf_op jit(solution)/shard_map/all_gather | solution.py:11
  878.4 385.0 %all-gather.36.cloned.1.call-start = ((), (), s32[]{:S(2)}) async-start(), calls=%async_computation.7 | async-start | bytes 4456448 | tf_op jit(solution)/shard_map/all_gather | solution.py:11
  879.0 461.7 %all-gather.46.cloned.1.call-start = ((), (), s32[]{:S(2)}) async-start(), calls=%async_computation.12 | async-start | bytes 4456448 | tf_op jit(solution)/shard_map/all_gather | solution.py:11
  1266.6 3.9 copy-start.1
Sparse Core Ops, SparseCore 0:
  10.2 78.7 all-gather.47
  160.1 7.6 all-gather.49
  170.6 77.2 all-gather.23
  250.5 74.6 all-gather.25
  327.8 74.6 all-gather.27
  405.2 74.6 all-gather.29
  482.6 74.6 all-gather.31
  560.1 74.6 all-gather.21
  637.6 74.6 all-gather.33
  720.6 74.6 all-gather.51
  866.1 7.6 all-gather.53
  876.6 77.2 all-gather.37
  956.6 74.6 all-gather.39
  1034.0 74.6 all-gather.41
  1111.3 74.6 all-gather.43
  1188.6 74.6 all-gather.35
  1266.0 74.6 all-gather.45
